TPU v7x, 512 devices: a whole 4x8x8 slice. The times are simulated.
512 devices in a mesh: row: 32 (over z_lo, y, core), col: 16 (over z_hi, x).
Axes of the slice: x: 4, y: 8, z: 8 (z_hi: 4, z_lo: 2; z = z_hi * 2 + z_lo), core: 2. Of those that a mesh axis runs over, the one named last changes fastest.
Arguments:
- phase: float32 [6, 524288], P(None, ('col', 'row')), may hold values from -6 to 6
- mass: float32 [524288], P(('col', 'row')), may hold values from 0.2 to 5
- active: int32 [4096], P(('row', 'col')), may hold values from 0 to 524287, as said below
Outputs:
- accels: float32 [3, 4096], P(None, ('row', 'col'))
- jerks: float32 [3, 4096], P(None, ('row', 'col'))
Inputs may be any that keep to these rules, and one draw needn't show every extreme that they name: `active`: the 4096 indices are distinct.
All inputs are finite; a program needn't handle non-finite values.
Results may differ from a plain program's by a relative error of at most 0.0003.
Values sent between devices are 32-bit elements; how exact they have to be, the bound alone decides.
A program may use at most 64 MiB of HBM per device.

v0:
```python
import math

import jax
import jax.numpy as jnp
from jax import lax
from jax.sharding import PartitionSpec as P

SOFTENING = 0.0001


def pair_terms(targets, src_phase, src_mass):
    offset = src_phase[0:3, None, :] - targets[0:3, :, None]
    vel_diff = src_phase[3:6, None, :] - targets[3:6, :, None]
    dist_sq = jnp.sum(offset * offset, axis=0) + SOFTENING
    inverse = lax.rsqrt(dist_sq)
    inverse_sq = inverse * inverse
    weight = src_mass[None, :] * inverse * inverse_sq
    radial = 3.0 * jnp.sum(offset * vel_diff, axis=0) * inverse_sq
    accels = jnp.sum(weight[None] * offset, axis=-1)
    jerks = jnp.sum(weight[None] * (vel_diff - radial[None] * offset), axis=-1)
    return (accels, jerks)


def select_stars(source, indices, first):
    columns = source.shape[1]
    offsets = indices - first
    inside = ((offsets >= 0) & (offsets < columns)).astype(jnp.float32)
    picked = jnp.take(source, jnp.clip(offsets, 0, columns - 1), axis=1)
    return picked * inside[None, :]


def sweep_sources(targets, src_phase, src_mass):
    columns = src_phase.shape[1]
    block_len = math.gcd(columns, 2048)

    def add_block(counter, carry):
        first = counter * block_len
        piece = lax.dynamic_slice_in_dim(src_phase, first, block_len, 1)
        masses = lax.dynamic_slice_in_dim(src_mass, first, block_len, 0)
        accels, jerks = pair_terms(targets, piece, masses)
        return (carry[0] + accels, carry[1] + jerks)

    zeros = jnp.zeros((3, targets.shape[1]), jnp.float32)
    return lax.fori_loop(0, columns // block_len, add_block, (zeros, zeros))


def shards(phase, mass, active):
    row_count = lax.axis_size("row")
    col_count = lax.axis_size("col")
    col_at = lax.axis_index("col")
    norming = 1.0 / (phase.shape[1] * row_count * col_count)
    block_ids = lax.all_gather(active, "col", axis=0, tiled=True)
    src_phase, src_mass = (
        lax.all_gather(phase, "row", axis=1, tiled=True),
        lax.all_gather(mass, "row", axis=0, tiled=True),
    )
    picked = select_stars(src_phase, block_ids, col_at * src_phase.shape[1])
    targets = lax.psum(picked, "col")
    accels, jerks = sweep_sources(targets, src_phase, src_mass)
    accels, jerks = (
        lax.psum_scatter(accels, "col", scatter_dimension=1, tiled=True),
        lax.psum_scatter(jerks, "col", scatter_dimension=1, tiled=True),
    )
    return (accels * norming, jerks * norming)


def solution(mesh):
    in_specs = (P(None, ("col", "row")), P(("col", "row")), P(("row", "col")))
    out_specs = (P(None, ("row", "col")), P(None, ("row", "col")))
    return jax.shard_map(shards, mesh=mesh, in_specs=in_specs, out_specs=out_specs, check_vma=False)
```

profile of v0, /device:TPU:1, one launch (start us, length us, event | category | flops | bytes accessed | tf_op | source)
XLA Modules:
  0.0 331.8 jit_solution(16159620314069810083)
XLA Ops:
  0.6 1.4 fusion.6
  3.5 20.5 %all-reduce = s32[128]{0:T(128)S(1)} all-reduce(s32[128]{0:T(128)S(1)} %dynamic-update-slice), channel_id=1, replica_groups=mesh['row'=32,'col'=16] {'col'}, use_global_device_ids=true, to_apply=%add | all-reduce | flops 128 | bytes 1024
  24.1 1.0 copy.11
  25.0 106.4 %all_gather.10 = f32[6,32768]{0,1:T(8,128)} all-gather(f32[6,1024]{0,1:T(8,128)S(1)} %copy.11), channel_id=1, replica_groups=mesh['row'=32,'col'=16] {'row'}, dimensions={1}, use_global_device_ids=true | all-gather | bytes 811008 | tf_op jit(solution)/shard_map/all_gather | solution.py:54
  131.5 6.4 %gather_fusion = f32[128,6]{1,0:T(8,128)S(1)} fusion(f32[6,32768]{0,1:T(8,128)} %all_gather.10, s32[1024]{0:T(1024)S(1)} %pad_clamp_fusion), kind=kCustom, calls=%fused_computation | custom fusion | bytes 6656 | tf_op jit(solution)/shard_map/jit(_take)/gather | solution.py:28
  138.0 63.3 %psum.7 = f32[6,128]{0,1:T(8,128)S(1)} all-reduce(f32[6,128]{0,1:T(8,128)S(1)} %multiply_bitcast_fusion), channel_id=1, replica_groups=mesh['row'=32,'col'=16] {'col'}, use_global_device_ids=true, to_apply=%region_0.1 | all-reduce | flops 768 | bytes 6144 | tf_op jit(solution)/shard_map/psum | solution.py:58
  201.3 9.9 %copy.12 = f32[6,32768]{1,0:T(8,128)S(1)} copy(f32[6,32768]{0,1:T(8,128)} %all_gather.10) | data formatting | bytes 1572864
  211.3 46.5 %all_gather.9 = f32[32768]{0:T(1024)S(1)} all-gather(f32[1024]{0:T(1024)S(1)} %copy-done), channel_id=1, replica_groups=mesh['row'=32,'col'=16] {'row'}, dimensions={0}, use_global_device_ids=true | all-gather | bytes 135168 | tf_op jit(solution)/shard_map/all_gather | solution.py:55
  257.8 40.6 %while.16 = (s32[]{:T(128)}, f32[3,128]{1,0:T(4,128)S(1)}, f32[3,128]{1,0:T(4,128)S(1)}, f32[32768]{0:T(1024)S(1)}, f32[6,32768]{1,0:T(8,128)S(1)}, /*index=5*/f...) while((s32[]{:T(128)}, f32[3,128]{1,0:T(4,128)S(1)}, ...), condition=%wide.region_6.7_spmd.clone, body=%wide.region_1.6_spmd.clone.sunk | while | flops 12059400 | bytes 8634557 | solution.py:44
  257.9 0.9 fusion.11
  259.1 1.2 fusion.12
  260.4 0.9 fusion.11
  261.6 1.2 fusion.12
  263.0 0.9 fusion.11
  264.2 1.2 fusion.12
  265.5 0.9 fusion.11
  266.7 1.2 fusion.12
  268.1 0.9 fusion.11
  269.2 1.2 fusion.12
  270.6 0.9 fusion.11
  271.8 1.2 fusion.12
  274.3 1.2 fusion.12
  276.9 1.2 fusion.12
  279.4 1.2 fusion.12
  281.9 1.2 fusion.12
  284.5 1.2 fusion.12
  287.0 1.2 fusion.12
  289.6 1.2 fusion.12
  292.1 1.2 fusion.12
  294.7 1.2 fusion.12
  297.2 1.2 fusion.12
  298.4 32.1 %all-reduce.3 = (f32[3,128]{1,0:T(4,128)S(1)}, f32[3,128]{1,0:T(4,128)S(1)}) all-reduce(f32[3,128]{1,0:T(4,128)S(1)} %get-tuple-element.112, f32[3,128]{1,0:T(4,128)S(1)} %get-tuple-element.113), channel_id=2, replica_groups=mesh['row'=32,'col'=16] {'col'}, use_global_device_ids=true, to_apply=%region_7.8.clone | all-reduce | flops 768 | bytes 6144
  (101 shorter events, 17.0 us)
Async XLA Ops:
  201.3 9.9 %copy-start = (f32[1024]{0:T(1024)S(1)}, f32[1024]{0:T(1024)}, u32[]{:S(2)}) copy-start(f32[1024]{0:T(1024)} %param.6) | copy-start | bytes 12292
where the time goes:
time: 338 us; the launch traced here: 332 us
  blocking collectives  269 us (80%)
  other arithmetic  38.7 us (11%)
  local copies, waits for them, and re-layouts  21.3 us (6%)
    all_gather x1, blocking collectives, shards(): lax.all_gather(phase, 'row', axis=1, tiled=True)  106 us
    psum x1, blocking collectives, shards(): targets = lax.psum(picked, 'col')  63.3 us
    unnamed x2, blocking collectives  52.6 us
    all_gather x1, blocking collectives, shards(): lax.all_gather(mass, 'row', axis=0, tiled=True)  46.5 us
    reduce_sum x16, other arithmetic, pair_terms(): jerks = jnp.sum(weight[None] * (vel_diff - radial[None] * offset), axis=-1)  19.2 us
    reduce_sum x16, other arithmetic, pair_terms(): radial = 3.0 * jnp.sum(offset * vel_diff, axis=0) * inverse_sq  13.7 us
    unnamed x7, local copies, waits for them, and re-layouts  13.2 us

commit v1 on v0

v1 whole, which is shorter than its diff:
```python
import functools

import jax
import jax.numpy as jnp
from jax import lax
from jax.experimental import pallas as pl
from jax.experimental.pallas import tpu as pltpu
from jax.sharding import PartitionSpec as P

SOFTENING = 0.0001
MESH = pl.DeviceIdType.MESH

NX, NY, NZ = 4, 8, 8
SRC_GROUP = NY * 2
TGT_GROUP = NX * NZ
STARS = 1024
TILES = STARS // 128
MINE = 8
PAIRS = TGT_GROUP // 2


def remote(src, dst, send, recv, device):
    return pltpu.make_async_remote_copy(
        src_ref=src, dst_ref=dst, send_sem=send, recv_sem=recv, device_id=device, device_id_type=MESH
    )


def kernel(
    norming, phase_ref, mass_ref, active_ref, acc_out, jerk_out,
    src, msrc, idx_x, idx_z, pick_x, pick_z, tgt, stage, part,
    own_sem, src_send, src_recv, mass_send, mass_recv, ix_send, ix_recv, iz_send, iz_recv,
    px_send, px_recv, pz_send, pz_recv, fin_send, fin_recv,
):
    r, c = lax.axis_index("row"), lax.axis_index("col")
    z_lo, b = r // 16, r % 16
    y, core = b // 2, b % 2
    z_hi, x = c // NX, c % NX
    z = z_hi * 2 + z_lo
    m = z_lo * 16 + c
    lane = lax.broadcasted_iota(jnp.int32, (8, 128), 1)

    def at_y(k, other):
        yy = (y + k) % NY
        cc = 1 - core if other else core
        return (z_lo * 16 + yy * 2 + cc, c)

    def at_x(k):
        return (r, z_hi * NX + (x + k) % NX)

    def at_z(k):
        zz = (z + k) % NZ
        return ((zz % 2) * 16 + b, (zz // 2) * NX + x)

    sources = [at_y(k, o) for o in (False, True) for k in range(NY) if o or k]
    partners = sources + [at_x(k) for k in range(1, NX)] + [at_z(k) for k in range(1, NZ)]
    barrier = pltpu.get_barrier_semaphore()
    for device in partners:
        pl.semaphore_signal(barrier, inc=1, device_id=device, device_id_type=MESH)

    own = [
        pltpu.make_async_copy(phase_ref, src.at[b], own_sem.at[0]),
        pltpu.make_async_copy(mass_ref, msrc.at[b], own_sem.at[1]),
    ]
    for copy in own:
        copy.start()
    idx_x[x] = jnp.zeros((8, 128), jnp.int32)
    idx_x[x, 0:1, 0:MINE] = active_ref[...]
    row = idx_x[x, 0:1, :]
    for shift in (8, 16, 32, 64):
        row = row + pltpu.roll(row, shift, 1)
    idx_x[x] = jnp.broadcast_to(row, (8, 128))

    pl.semaphore_wait(barrier, len(partners))

    sends = []

    def go(copy):
        copy.start()
        sends.append(copy)

    for n, k in enumerate((4, 3, 5, 2, 6, 1, 7)):
        go(remote(phase_ref, src.at[b], src_send.at[n], src_recv.at[b], at_y(k, False)))
    go(remote(phase_ref, src.at[b], src_send.at[7], src_recv.at[b], at_y(0, True)))
    for k in range(1, NX):
        go(remote(idx_x.at[x], idx_x.at[x], ix_send.at[k], ix_recv.at[x], at_x(k)))
    for n, device in enumerate(sources):
        go(remote(mass_ref, msrc.at[b], mass_send.at[n], mass_recv.at[b], device))

    merged = jnp.where((lane // 8) % NX == x, idx_x[x], 0)
    for k in range(1, NX):
        xx = (x + k) % NX
        remote(idx_x.at[xx], idx_x.at[xx], ix_send.at[0], ix_recv.at[xx], at_x(k)).wait_recv()
        merged = jnp.where((lane // 8) % NX == xx, idx_x[xx], merged)
    idx_z[z] = merged
    for k in range(1, NZ):
        go(remote(idx_z.at[z], idx_z.at[z], iz_send.at[k], iz_recv.at[z], at_z(k)))

    for n, k in enumerate((1, 7, 2, 6, 3, 5, 4)):
        bb = ((y + k) % NY) * 2 + core
        remote(phase_ref, src.at[bb], src_send.at[0], src_recv.at[bb], at_y(k, False)).wait_recv()
        go(remote(src.at[bb], src.at[bb], src_send.at[8 + n], src_recv.at[bb], at_y(0, True)))
    for k in range(1, NZ):
        zz = (z + k) % NZ
        remote(idx_z.at[zz], idx_z.at[zz], iz_send.at[0], iz_recv.at[zz], at_z(k)).wait_recv()
    base = (c * 32 + z_lo * 16) * STARS
    offset = []
    for q in range(2):
        index = jnp.zeros((8, 128), jnp.int32)
        for h in range(NZ // 2):
            index = jnp.where(lane // 32 == h, idx_z[h * 2 + q], index)
        offset.append(index - base)
    for copy in own:
        copy.wait()
    for k in range(NY):
        bb = ((y + k) % NY) * 2 + 1 - core
        remote(phase_ref, src.at[bb], src_send.at[0], src_recv.at[bb], at_y(0, True)).wait_recv()

    within = [o % 128 for o in offset]
    tile = [lax.shift_right_arithmetic(o, 7) for o in offset]

    def pick(bb, found):
        found = list(found)
        for k in range(TILES):
            piece = src[bb, :, k * 128:(k + 1) * 128]
            for q in range(2):
                values = jnp.take_along_axis(piece, within[q][:6], axis=1)
                found[q] = jnp.where(tile[q][:6] == bb * TILES + k, values, found[q])
        return tuple(found)

    nothing = jnp.zeros((6, 128), jnp.float32)
    found = lax.fori_loop(0, SRC_GROUP, pick, (nothing, nothing))
    for q in range(2):
        pick_x[x, q] = found[q]
    for k in range(1, NX):
        go(remote(pick_x.at[x], pick_x.at[x], px_send.at[k], px_recv.at[x], at_x(k)))
    total = list(found)
    for k in range(1, NX):
        xx = (x + k) % NX
        remote(pick_x.at[xx], pick_x.at[xx], px_send.at[0], px_recv.at[xx], at_x(k)).wait_recv()
        for q in range(2):
            total[q] = total[q] + pick_x[xx, q]
    for q in range(2):
        pick_z[z, q] = total[q]
    for k in range(1, NZ):
        go(remote(pick_z.at[z], pick_z.at[z], pz_send.at[k], pz_recv.at[z], at_z(k)))
    for k in (1, 7, 2, 6, 3, 5, 4):
        zz = (z + k) % NZ
        remote(pick_z.at[zz], pick_z.at[zz], pz_send.at[0], pz_recv.at[zz], at_z(k)).wait_recv()
        for q in range(2):
            total[q] = total[q] + pick_z[zz, q]
    for q in range(2):
        turned = jnp.concatenate([total[q], jnp.zeros((2, 128), jnp.float32)], axis=0).T
        for k in range(6):
            tgt[k, q * 128:(q + 1) * 128, :] = jnp.broadcast_to(turned[:, k:k + 1], (128, 128))
    for n in range(15):
        k, other = (n + 1, False) if n < 7 else (n - 7, True)
        bb = ((y + k) % NY) * 2 + (1 - core if other else core)
        remote(mass_ref, msrc.at[bb], mass_send.at[0], mass_recv.at[bb], at_y(k, other)).wait_recv()

    def block(i, carry):
        step = i // 2
        zz = (z + 4 + (1 - 2 * (step % 2)) * ((step + 1) // 2)) % NZ
        half = (x // 2 + 1 + i) % 2
        p = (zz % 2) * 8 + (zz // 2) * 2 + half
        first = pl.multiple_of(p * 16, 16)
        here = [[tgt[k, pl.ds(first + 8 * g, 8), :] for k in range(6)] for g in range(2)]

        def sweep(bb, sums):
            sums = [list(s) for s in sums]
            for k in range(TILES):
                star = [jnp.broadcast_to(src[bb, n:n + 1, k * 128:(k + 1) * 128], (8, 128)) for n in range(6)]
                heft = jnp.broadcast_to(msrc[bb, k:k + 1, :], (8, 128))
                for g in range(2):
                    dx, dy, dz, du, dv, dw = (star[n] - here[g][n] for n in range(6))
                    dist_sq = (dx * dx + dy * dy + dz * dz) + SOFTENING
                    inverse = lax.rsqrt(dist_sq)
                    inverse_sq = inverse * inverse
                    weight = heft * inverse * inverse_sq
                    radial = 3.0 * (dx * du + dy * dv + dz * dw) * inverse_sq
                    s = sums[g]
                    s[0] += weight * dx
                    s[1] += weight * dy
                    s[2] += weight * dz
                    s[3] += weight * (du - radial * dx)
                    s[4] += weight * (dv - radial * dy)
                    s[5] += weight * (dw - radial * dz)
            return tuple(tuple(s) for s in sums)

        zero = jnp.zeros((8, 128), jnp.float32)
        sums = lax.fori_loop(0, SRC_GROUP, sweep, ((zero,) * 6,) * 2)
        for g in range(2):
            out = zero
            for n in range(6):
                out = jnp.where(lane == n, jnp.sum(sums[g][n], axis=1, keepdims=True), out)
            member = p * 2 + g
            stage[member] = out

            @pl.when(member != m)
            def _():
                device = ((zz % 2) * 16 + b, (zz // 2) * NX + half * 2 + g)
                remote(stage.at[member], part.at[m], fin_send.at[member], fin_recv.at[m], device).start()

        return carry

    lax.fori_loop(0, PAIRS, block, 0)

    def gather(k, carry):
        member = (m + k) % TGT_GROUP
        remote(stage.at[member], part.at[member], fin_send.at[member], fin_recv.at[member], at_x(1)).wait()
        return carry

    lax.fori_loop(1, TGT_GROUP, gather, 0)
    out = stage[m]
    for k in range(1, TGT_GROUP):
        out = out + part[(m + k) % TGT_GROUP]
    turned = (out * norming).T
    acc_out[...] = turned[0:3, :]
    jerk_out[...] = turned[3:6, :]
    for copy in sends:
        copy.wait_send()


def shards(phase, mass, active):
    count = phase.shape[1] * lax.axis_size("row") * lax.axis_size("col")
    vmem = pl.BlockSpec(memory_space=pltpu.VMEM)
    hbm = pl.BlockSpec(memory_space=pl.ANY)
    dma = pltpu.SemaphoreType.DMA
    out = jax.ShapeDtypeStruct((3, MINE), jnp.float32)
    return pl.pallas_call(
        functools.partial(kernel, 1.0 / count),
        out_shape=(out, out),
        in_specs=[hbm, hbm, vmem],
        out_specs=(vmem, vmem),
        scratch_shapes=[
            pltpu.VMEM((SRC_GROUP, 6, STARS), jnp.float32),
            pltpu.VMEM((SRC_GROUP, TILES, 128), jnp.float32),
            pltpu.VMEM((NX, 8, 128), jnp.int32),
            pltpu.VMEM((NZ, 8, 128), jnp.int32),
            pltpu.VMEM((NX, 2, 6, 128), jnp.float32),
            pltpu.VMEM((NZ, 2, 6, 128), jnp.float32),
            pltpu.VMEM((6, TGT_GROUP * MINE, 128), jnp.float32),
            pltpu.VMEM((TGT_GROUP, 8, 128), jnp.float32),
            pltpu.VMEM((TGT_GROUP, 8, 128), jnp.float32),
            dma((2,)),
            dma((15,)),
            dma((SRC_GROUP,)),
            dma((15,)),
            dma((SRC_GROUP,)),
            dma((NX,)),
            dma((NX,)),
            dma((NZ,)),
            dma((NZ,)),
            dma((NX,)),
            dma((NX,)),
            dma((NZ,)),
            dma((NZ,)),
            dma((TGT_GROUP,)),
            dma((TGT_GROUP,)),
        ],
        compiler_params=pltpu.CompilerParams(collective_id=0, has_side_effects=True),
    )(phase, mass.reshape(TILES, 128), active.reshape(1, MINE))


def solution(mesh):
    in_specs = (P(None, ("col", "row")), P(("col", "row")), P(("row", "col")))
    out_specs = (P(None, ("row", "col")), P(None, ("row", "col")))
    return jax.shard_map(shards, mesh=mesh, in_specs=in_specs, out_specs=out_specs, check_vma=False)
```

time: 338 us -> 67.6 us (0.20); the launches traced: 332 us -> 67.4 us
  blocking collectives: 269 us -> 0 us
  Pallas kernels: 0 us -> 64.9 us
  other arithmetic: 38.7 us -> 0 us
  local copies, waits for them, and re-layouts: 21.3 us -> 1.89 us
    all_gather x2 -> x0, blocking collectives: 153 us -> none  [the longest x1 106 us: shards(): lax.all_gather(phase, 'row', axis=1, tiled=True)]
    pallas_call x0 -> x1, Pallas kernels: none -> 64.9 us  [shards(): pl.pallas_call(functools.partial(kernel, 1.0 / count), out_shape=(out, ou...]
    psum x1 -> x0, blocking collectives: 63.3 us -> none  [shards(): targets = lax.psum(picked, 'col')]
    unnamed x2 -> x0, blocking collectives: 52.6 us -> none
    reduce_sum x32 -> x0, other arithmetic: 32.9 us -> none  [the longest x16 19.2 us: pair_terms(): jerks = jnp.sum(weight[None] * (vel_diff - radial[None] * offset), axis=-1)]
    unnamed x7 -> x6, local copies, waits for them, and re-layouts: 13.2 us -> 1.89 us
    gather x1 -> x0, local copies, waits for them, and re-layouts: 6.42 us -> none  [select_stars(): picked = jnp.take(source, jnp.clip(offsets, 0, columns - 1), axis=1)]
    mul x18 -> x0, other arithmetic: 5.53 us -> none  [the longest x16 4.78 us: pair_terms(): weight = src_mass[None, :] * inverse * inverse_sq]
where the time goes in v1:
time: 67.6 us; the launch traced here: 67.4 us
  Pallas kernels  64.9 us (96%)
  local copies, waits for them, and re-layouts  1.89 us (3%)
    pallas_call x1, Pallas kernels, shards(): pl.pallas_call(functools.partial(kernel, 1.0 / count), out_shape=(out, ou...  64.9 us
    unnamed x6, local copies, waits for them, and re-layouts  1.89 us

profile of v1, /device:TPU:1, one launch (start us, length us, event | category | flops | bytes accessed | tf_op | source)
XLA Modules:
  0.0 67.4 jit_solution(13964629513002580546)
XLA Ops:
  0.6 64.9 %shard_map.50 = (f32[3,8]{1,0:T(4,128)}, f32[3,8]{1,0:T(4,128)}) custom-call(f32[6,1024]{1,0:T(8,128)} %phase_ref.1, f32[8,128]{1,0:T(8,128)} %bitcast.2, s32[1,8]{1,0:T(1,128)} %bitcast.3), custom_call_target="tpu_custom_call" | custom-call | tf_op jit(solution)/shard_map/pallas_call | solution.py:229
  65.5 0.0 copy-start.1
  65.5 0.7 copy-done.1
  66.2 0.0 copy-start
  66.2 0.6 copy.7
  66.8 0.1 copy-done
  66.8 0.6 copy.8
Async XLA Ops:
  65.5 0.7 copy-start.1
  66.2 0.7 copy-start

commit v2 on v1

v2 whole, which is shorter than its diff:
```python
import jax
import jax.numpy as jnp
from jax import lax
from jax.experimental import pallas as pl
from jax.experimental.pallas import tpu as pltpu
from jax.sharding import PartitionSpec as P

SOFTENING = 0.0001
MESH = pl.DeviceIdType.MESH

NX, NY, NZ = 4, 8, 8
SRC_GROUP = NX * 2 * 2
TGT_GROUP = NY // 2 * NZ
STARS = 1024
TILES = STARS // 128
MINE = 8
PAIRS = TGT_GROUP // 2


def remote(src, dst, send, recv, device):
    return pltpu.make_async_remote_copy(
        src_ref=src, dst_ref=dst, send_sem=send, recv_sem=recv, device_id=device, device_id_type=MESH
    )


def kernel(
    phase_ref, mass_ref, active_ref, out_ref,
    src, msrc, ids, idx, pick, tgt, stage, part,
    own_sem, src_send, src_recv, mass_send, mass_recv, idx_send, idx_recv, pick_send, pick_recv, fin_send, fin_recv,
):
    r, c = lax.axis_index("row"), lax.axis_index("col")
    z_lo, y, core = r // 16, r // 2 % 8, r % 2
    z_hi, x = c // NX, c % NX
    z, y_hi, y_lo = z_hi * 2 + z_lo, y // 2, y % 2
    b = x * 4 + y_lo * 2 + core
    m = y_hi * NZ + z
    lane = lax.broadcasted_iota(jnp.int32, (8, 128), 1)

    def place(xx, yy, zz, cc):
        return ((zz % 2) * 16 + yy * 2 + cc, (zz // 2) * NX + xx)

    def source(dx, dy, dc):
        xx, yl, cc = (x + dx) % NX, (y_lo + dy) % 2, (core + dc) % 2
        return place(xx, y_hi * 2 + yl, z, cc), xx * 4 + yl * 2 + cc

    def target(dy, dz):
        yh, zz = (y_hi + dy) % (NY // 2), (z + dz) % NZ
        return place(x, yh * 2 + y_lo, zz, core), yh * NZ + zz

    near = [source(dx, dy, 0) for dx, dy in ((2, 1), (1, 1), (3, 1), (2, 0), (1, 0), (3, 0), (0, 1))]
    twin, twin_block = source(0, 0, 1)
    beyond = [source(dx, dy, 1) for dx, dy in ((2, 1), (1, 1), (3, 1), (2, 0), (1, 0), (3, 0), (0, 1))]
    fellows = [target(dy, dz) for dy in (2, 1, 3, 0) for dz in (4, 3, 5, 2, 6, 1, 7, 0) if dy or dz]
    partners = [d for d, _ in near + beyond + fellows] + [twin]
    barrier = pltpu.get_barrier_semaphore()
    for device in partners:
        pl.semaphore_signal(barrier, inc=1, device_id=device, device_id_type=MESH)

    own = [
        pltpu.make_async_copy(active_ref, ids, own_sem.at[0]),
        pltpu.make_async_copy(phase_ref, src.at[b], own_sem.at[1]),
        pltpu.make_async_copy(mass_ref, msrc.at[b], own_sem.at[2]),
    ]
    for copy in own:
        copy.start()
    own[0].wait()
    idx[m] = jnp.zeros((1, 128), jnp.int32)
    idx[m, :, 0:MINE] = ids[...]
    row = idx[m]
    for shift in (8, 16, 32, 64):
        row = row + pltpu.roll(row, shift, 1)
    idx[m] = row

    pl.semaphore_wait(barrier, len(partners))

    sends = []

    def go(copy):
        copy.start()
        sends.append(copy)

    for n, (device, _) in enumerate(near + [(twin, 0)]):
        go(remote(phase_ref, src.at[b], src_send.at[n], src_recv.at[b], device))
    for n, (device, _) in enumerate(fellows):
        go(remote(idx.at[m], idx.at[m], idx_send.at[n], idx_recv.at[m], device))
    for n, (device, _) in enumerate(near + beyond + [(twin, 0)]):
        go(remote(mass_ref, msrc.at[b], mass_send.at[n], mass_recv.at[b], device))

    for n in (6, 5, 4, 3, 2, 1, 0):
        device, bb = near[n]
        remote(phase_ref, src.at[bb], src_send.at[0], src_recv.at[bb], device).wait_recv()
        go(remote(src.at[bb], src.at[bb], src_send.at[8 + n], src_recv.at[bb], twin))
    for device, mm in fellows:
        remote(idx.at[mm], idx.at[mm], idx_send.at[0], idx_recv.at[mm], device).wait_recv()

    within, tile = [], []
    for q in range(2):
        index = jnp.zeros((8, 128), jnp.int32)
        for g in range(16):
            index = jnp.where(lane // MINE == g, jnp.broadcast_to(idx[q * 16 + g], (8, 128)), index)
        index = index[:6]
        block = index // STARS
        here = (block // 128 == z_hi) & (block // 16 % 2 == z_lo) & (block // 4 % 4 == y_hi)
        within.append(index % 128)
        tile.append(jnp.where(here, (block // 32 % 4 * 4 + block % 4) * TILES + index // 128 % TILES, -1))
    for copy in own[1:]:
        copy.wait()
    for device, bb in [(twin, twin_block)] + beyond[::-1]:
        remote(phase_ref, src.at[bb], src_send.at[0], src_recv.at[bb], twin).wait_recv()

    def choose(bb, found):
        found = list(found)
        for k in range(TILES):
            piece = src[bb, :, k * 128:(k + 1) * 128]
            for q in range(2):
                values = jnp.take_along_axis(piece, within[q], axis=1)
                found[q] = jnp.where(tile[q] == bb * TILES + k, values, found[q])
        return tuple(found)

    nothing = jnp.zeros((6, 128), jnp.float32)
    found = lax.fori_loop(0, SRC_GROUP, choose, (nothing, nothing))
    for q in range(2):
        pick[m, q] = found[q]
    for n, (device, _) in enumerate(fellows):
        go(remote(pick.at[m], pick.at[m], pick_send.at[n], pick_recv.at[m], device))
    for n, (device, bb) in enumerate(near + beyond + [(twin, twin_block)]):
        remote(mass_ref, msrc.at[bb], mass_send.at[0], mass_recv.at[bb], device).wait_recv()
    total = list(found)
    for device, mm in fellows[::-1]:
        remote(pick.at[mm], pick.at[mm], pick_send.at[0], pick_recv.at[mm], device).wait_recv()
        for q in range(2):
            total[q] = total[q] + pick[mm, q]
    for q in range(2):
        turned = jnp.concatenate([total[q], jnp.zeros((2, 128), jnp.float32)], axis=0).T
        for k in range(6):
            tgt[k, q * 128:(q + 1) * 128, :] = jnp.broadcast_to(turned[:, k:k + 1], (128, 128))

    def block(i, carry):
        def far(j):
            return 2 + j // 2 - (j % 2) * (1 + 2 * (j // 2))

        yh, zp = (y_hi + far(i // 4)) % 4, (z // 2 + far(i % 4)) % 4
        p = yh * 4 + zp
        first = pl.multiple_of(p * 16, 16)
        here = [[tgt[k, pl.ds(first + 8 * g, 8), :] for k in range(6)] for g in range(2)]

        def sweep(bb, sums):
            sums = [list(s) for s in sums]
            for k in range(TILES):
                star = [jnp.broadcast_to(src[bb, n:n + 1, k * 128:(k + 1) * 128], (8, 128)) for n in range(6)]
                heft = jnp.broadcast_to(msrc[bb, k:k + 1, :], (8, 128))
                for g in range(2):
                    dx, dy, dz, du, dv, dw = (star[n] - here[g][n] for n in range(6))
                    dist_sq = (dx * dx + dy * dy + dz * dz) + SOFTENING
                    inverse = lax.rsqrt(dist_sq)
                    inverse_sq = inverse * inverse
                    weight = heft * inverse * inverse_sq
                    radial = 3.0 * (dx * du + dy * dv + dz * dw) * inverse_sq
                    s = sums[g]
                    s[0] += weight * dx
                    s[1] += weight * dy
                    s[2] += weight * dz
                    s[3] += weight * (du - radial * dx)
                    s[4] += weight * (dv - radial * dy)
                    s[5] += weight * (dw - radial * dz)
            return tuple(tuple(s) for s in sums)

        zero = jnp.zeros((8, 128), jnp.float32)
        sums = lax.fori_loop(0, SRC_GROUP, sweep, ((zero,) * 6,) * 2)
        for g in range(2):
            out = zero
            for n in range(6):
                out = jnp.where(lane == n, jnp.sum(sums[g][n], axis=1, keepdims=True), out)
            member = p * 2 + g
            stage[member] = out

            @pl.when(member != m)
            def _():
                device = place(x, yh * 2 + y_lo, zp * 2 + g, core)
                remote(stage.at[member], part.at[m], fin_send.at[member], fin_recv.at[m], device).start()

        return carry

    lax.fori_loop(0, PAIRS, block, 0)

    def gather(k, carry):
        member = (m + k) % TGT_GROUP
        remote(stage.at[member], part.at[member], fin_send.at[member], fin_recv.at[member], twin).wait()
        return carry

    lax.fori_loop(1, TGT_GROUP, gather, 0)
    out = stage[m]
    for k in range(1, TGT_GROUP):
        out = out + part[(m + k) % TGT_GROUP]
    out_ref[...] = out.T[0:8, :]
    for copy in sends:
        copy.wait_send()


def shards(phase, mass, active):
    norming = 1.0 / (phase.shape[1] * lax.axis_size("row") * lax.axis_size("col"))
    vmem = pl.BlockSpec(memory_space=pltpu.VMEM)
    hbm = pl.BlockSpec(memory_space=pl.ANY)
    dma = pltpu.SemaphoreType.DMA
    sums = pl.pallas_call(
        kernel,
        out_shape=jax.ShapeDtypeStruct((8, MINE), jnp.float32),
        in_specs=[hbm, hbm, hbm],
        out_specs=vmem,
        scratch_shapes=[
            pltpu.VMEM((SRC_GROUP, 6, STARS), jnp.float32),
            pltpu.VMEM((SRC_GROUP, TILES, 128), jnp.float32),
            pltpu.VMEM((1, MINE), jnp.int32),
            pltpu.VMEM((TGT_GROUP, 1, 128), jnp.int32),
            pltpu.VMEM((TGT_GROUP, 2, 6, 128), jnp.float32),
            pltpu.VMEM((6, TGT_GROUP * MINE, 128), jnp.float32),
            pltpu.VMEM((TGT_GROUP, 8, 128), jnp.float32),
            pltpu.VMEM((TGT_GROUP, 8, 128), jnp.float32),
            dma((3,)),
            dma((15,)),
            dma((SRC_GROUP,)),
            dma((15,)),
            dma((SRC_GROUP,)),
            dma((TGT_GROUP,)),
            dma((TGT_GROUP,)),
            dma((TGT_GROUP,)),
            dma((TGT_GROUP,)),
            dma((TGT_GROUP,)),
            dma((TGT_GROUP,)),
        ],
        compiler_params=pltpu.CompilerParams(collective_id=0, has_side_effects=True),
    )(phase, mass.reshape(TILES, 128), active.reshape(1, MINE))
    return sums[0:3] * norming, sums[3:6] * norming


def solution(mesh):
    in_specs = (P(None, ("col", "row")), P(("col", "row")), P(("row", "col")))
    out_specs = (P(None, ("row", "col")), P(None, ("row", "col")))
    return jax.shard_map(shards, mesh=mesh, in_specs=in_specs, out_specs=out_specs, check_vma=False)
```

time: 67.6 us -> 69.7 us (1.031)
  the two profiles are of different devices: /device:TPU:1 before, /device:TPU:2 now
where the time goes in v2:
time: 69.7 us; the launch traced here: 69.5 us
  Pallas kernels  67.5 us (97%)
  other arithmetic  1.33 us (2%)
    pallas_call x1, Pallas kernels, shards(): pl.pallas_call(kernel, out_shape=jax.ShapeDtypeStruct((8, MINE), jnp.floa...  67.5 us

profile of v2, /device:TPU:2, one launch (start us, length us, event | category | flops | bytes accessed | tf_op | source)
XLA Modules:
  0.0 69.5 jit_solution(17704476439877057332)
XLA Ops:
  0.6 67.5 %shard_map.50 = f32[8,8]{1,0:T(8,128)} custom-call(f32[6,1024]{1,0:T(8,128)} %phase_ref.1, f32[8,128]{1,0:T(8,128)} %bitcast.2, s32[1,8]{1,0:T(1,128)} %bitcast.3), custom_call_target="tpu_custom_call" | custom-call | tf_op jit(solution)/shard_map/pallas_call | solution.py:205
  68.2 1.3 %slice_multiply_fusion = (f32[3,8]{1,0:T(4,128)}, f32[3,8]{1,0:T(4,128)}) fusion(f32[8,8]{1,0:T(8,128)} %shard_map.50), kind=kLoop, calls=%fused_computation | loop fusion | flops 48 | bytes 384 | tf_op jit(solution)/shard_map/mul | solution.py:233

commit v3 on v2

v3 whole, which is shorter than its diff:
```python
import jax
import jax.numpy as jnp
from jax import lax
from jax.experimental import pallas as pl
from jax.experimental.pallas import tpu as pltpu
from jax.sharding import PartitionSpec as P

SOFTENING = 0.0001
MESH = pl.DeviceIdType.MESH

NX, NY, NZ = 4, 8, 8
SRC_GROUP = NY * 2
TGT_GROUP = NX * NZ
STARS = 1024
TILES = STARS // 128
MINE = 8
PAIRS = TGT_GROUP // 2


def remote(src, dst, send, recv, device):
    return pltpu.make_async_remote_copy(
        src_ref=src, dst_ref=dst, send_sem=send, recv_sem=recv, device_id=device, device_id_type=MESH
    )


def kernel(
    phase_ref, mass_ref, active_ref, out_ref,
    src, msrc, ids, idx_x, idx_z, pick_x, pick_z, tgt, raw, stage, part,
    own_sem, src_send, src_recv, mass_send, mass_recv, ix_send, ix_recv, iz_send, iz_recv,
    px_send, px_recv, pz_send, pz_recv, fin_send, fin_recv,
):
    r, c = lax.axis_index("row"), lax.axis_index("col")
    z_lo, b = r // 16, r % 16
    y, core = b // 2, b % 2
    z_hi, x = c // NX, c % NX
    z = z_hi * 2 + z_lo
    m = z_lo * 16 + c
    slot = core * NX + x
    lane = lax.broadcasted_iota(jnp.int32, (8, 128), 1)

    def along_y(k, dc):
        bb = (y + k) % NY * 2 + (core + dc) % 2
        return (z_lo * 16 + bb, c), bb

    def along_x(k, dc):
        xx, cc = (x + k) % NX, (core + dc) % 2
        return (z_lo * 16 + y * 2 + cc, z_hi * NX + xx), cc * NX + xx

    def along_z(k):
        zz = (z + k) % NZ
        return (zz % 2 * 16 + b, zz // 2 * NX + x), zz

    near = [along_y(k, 0) for k in (4, 3, 5, 2, 6, 1, 7)]
    beyond = [along_y(k, 1) for k in (4, 3, 5, 2, 6, 1, 7)]
    twin, twin_block = along_y(0, 1)
    across = [along_x(k, dc) for k, dc in ((2, 1), (2, 0), (1, 1), (3, 1), (1, 0), (3, 0), (0, 1))]
    fellows = [along_z(k) for k in (4, 3, 5, 2, 6, 1, 7)]
    partners = [d for d, _ in near + beyond + across + fellows]
    barrier = pltpu.get_barrier_semaphore()
    for device in partners:
        pl.semaphore_signal(barrier, inc=1, device_id=device, device_id_type=MESH)

    own = [
        pltpu.make_async_copy(active_ref, ids, own_sem.at[0]),
        pltpu.make_async_copy(phase_ref, src.at[b], own_sem.at[1]),
        pltpu.make_async_copy(mass_ref, msrc.at[b], own_sem.at[2]),
    ]
    for copy in own:
        copy.start()
    own[0].wait()
    idx_x[slot] = jnp.zeros((8, 128), jnp.int32)
    idx_x[slot, 0:1, 0:MINE] = ids[...]
    row = idx_x[slot, 0:1, :]
    for shift in (8, 16, 32, 64):
        row = row + pltpu.roll(row, shift, 1)
    idx_x[slot] = jnp.broadcast_to(row, (8, 128))

    pl.semaphore_wait(barrier, len(partners))

    sends = []

    def go(copy):
        copy.start()
        sends.append(copy)

    for n, (device, _) in enumerate(near):
        go(remote(phase_ref, src.at[b], src_send.at[n], src_recv.at[b], device))
    for n, (device, _) in enumerate(across):
        go(remote(idx_x.at[slot], idx_x.at[slot], ix_send.at[n], ix_recv.at[slot], device))
    go(remote(phase_ref, src.at[b], src_send.at[7], src_recv.at[b], twin))
    for n, (device, _) in enumerate(near + beyond + [(twin, 0)]):
        go(remote(mass_ref, msrc.at[b], mass_send.at[n], mass_recv.at[b], device))

    for device, ss in across:
        remote(idx_x.at[ss], idx_x.at[ss], ix_send.at[0], ix_recv.at[ss], device).wait_recv()
    sublane = lax.broadcasted_iota(jnp.int32, (8, 128), 0)
    merged = jnp.zeros((8, 128), jnp.int32)
    for cc in range(2):
        for xx in range(NX):
            chosen = (lane // MINE % NX == xx) & ((sublane == 0) == (cc == 0))
            merged = jnp.where(chosen, idx_x[cc * NX + xx], merged)
    idx_z[z] = merged
    for n, (device, _) in enumerate(fellows):
        go(remote(idx_z.at[z], idx_z.at[z], iz_send.at[n], iz_recv.at[z], device))
    for device, zz in fellows:
        remote(idx_z.at[zz], idx_z.at[zz], iz_send.at[0], iz_recv.at[zz], device).wait_recv()

    base = (c * 32 + z_lo * 16) * STARS
    within, tile = [], []
    for cc in range(2):
        for q in range(2):
            index = jnp.zeros((6, 128), jnp.int32)
            for h in range(NZ // 2):
                ids_h = jnp.broadcast_to(idx_z[h * 2 + q, cc:cc + 1, :], (6, 128))
                index = jnp.where(lane[:6] // 32 == h, ids_h, index)
            within.append((index - base) % 128)
            tile.append(lax.shift_right_arithmetic(index - base, 7))

    for n in (5, 6, 3, 4, 1, 2, 0):
        device, bb = near[n]
        remote(phase_ref, src.at[bb], src_send.at[0], src_recv.at[bb], device).wait_recv()
        go(remote(src.at[bb], src.at[bb], src_send.at[8 + n], src_recv.at[bb], twin))
    for copy in own[1:]:
        copy.wait()

    def choose(yy, found):
        found = list(found)
        bb = yy * 2 + core
        for k in range(TILES):
            piece = src[bb, :, k * 128:(k + 1) * 128]
            for n in range(4):
                values = jnp.take_along_axis(piece, within[n], axis=1)
                found[n] = jnp.where(tile[n] == bb * TILES + k, values, found[n])
        return tuple(found)

    found = lax.fori_loop(0, NY, choose, (jnp.zeros((6, 128), jnp.float32),) * 4)
    for n in range(4):
        pick_x[n // 2, slot, n % 2] = found[n]
    for n, (device, ss) in enumerate(across):
        cc = ss // NX
        go(remote(pick_x.at[cc, slot], pick_x.at[cc, slot], px_send.at[n], px_recv.at[slot], device))
    total = [pick_x[core, slot, q] for q in range(2)]
    for device, ss in across[::-1]:
        remote(pick_x.at[core, ss], pick_x.at[core, ss], px_send.at[0], px_recv.at[ss], device).wait_recv()
        for q in range(2):
            total[q] = total[q] + pick_x[core, ss, q]
    for q in range(2):
        pick_z[z, q] = total[q]
    for n, (device, _) in enumerate(fellows):
        go(remote(pick_z.at[z], pick_z.at[z], pz_send.at[n], pz_recv.at[z], device))
    for device, bb in [(twin, twin_block)] + beyond:
        remote(phase_ref, src.at[bb], src_send.at[0], src_recv.at[bb], twin).wait_recv()
    for device, bb in near + beyond + [(twin, twin_block)]:
        remote(mass_ref, msrc.at[bb], mass_send.at[0], mass_recv.at[bb], device).wait_recv()
    for device, zz in fellows[::-1]:
        remote(pick_z.at[zz], pick_z.at[zz], pz_send.at[0], pz_recv.at[zz], device).wait_recv()
        for q in range(2):
            total[q] = total[q] + pick_z[zz, q]
    for q in range(2):
        turned = jnp.concatenate([total[q], jnp.zeros((2, 128), jnp.float32)], axis=0).T
        for k in range(6):
            tgt[k, q * 128:(q + 1) * 128, :] = jnp.broadcast_to(turned[:, k:k + 1], (128, 128))

    def pair(i):
        step = i // 2
        zz = (z + 4 + (1 - 2 * (step % 2)) * ((step + 1) // 2)) % NZ
        half = (x // 2 + 1 + i) % 2
        return zz, half, zz % 2 * 8 + zz // 2 * 2 + half

    def reduce(p):
        for g in range(2):
            out = jnp.zeros((8, 128), jnp.float32)
            for n in range(6):
                out = jnp.where(lane == n, jnp.sum(raw[g, n], axis=1, keepdims=True), out)
            stage[p * 2 + g] = out

    def hand_over(zz, half, p, g):
        device = (zz % 2 * 16 + b, zz // 2 * NX + half * 2 + g)
        remote(stage.at[p * 2 + g], part.at[m], fin_send.at[p * 2 + g], fin_recv.at[m], device).start()

    def block(i, carry):
        p = pair(i)[2]
        before = pair(jnp.maximum(i - 1, 0))
        first = pl.multiple_of(p * 16, 16)
        here = [[tgt[k, pl.ds(first + 8 * g, 8), :] for k in range(6)] for g in range(2)]
        reduce(before[2])
        zero = jnp.zeros((8, 128), jnp.float32)
        sums = [[zero] * 6, [zero] * 6]
        for t in range(SRC_GROUP * TILES):
            bb, k = t // TILES, t % TILES
            star = [jnp.broadcast_to(src[bb, n:n + 1, k * 128:(k + 1) * 128], (8, 128)) for n in range(6)]
            heft = jnp.broadcast_to(msrc[bb, k:k + 1, :], (8, 128))
            for g in range(2):
                dx, dy, dz, du, dv, dw = (star[n] - here[g][n] for n in range(6))
                dist_sq = (dx * dx + dy * dy + dz * dz) + SOFTENING
                inverse = lax.rsqrt(dist_sq)
                inverse_sq = inverse * inverse
                weight = heft * inverse * inverse_sq
                radial = 3.0 * (dx * du + dy * dv + dz * dw) * inverse_sq
                s = sums[g]
                s[0] += weight * dx
                s[1] += weight * dy
                s[2] += weight * dz
                s[3] += weight * (du - radial * dx)
                s[4] += weight * (dv - radial * dy)
                s[5] += weight * (dw - radial * dz)
        for g in range(2):
            for n in range(6):
                raw[g, n] = sums[g][n]

        @pl.when(i > 0)
        def _():
            for g in range(2):
                hand_over(*before, g)

        return carry

    raw[...] = jnp.zeros_like(raw)
    lax.fori_loop(0, PAIRS, block, 0)
    zz, half, p = pair(PAIRS - 1)
    reduce(p)
    for g in range(2):
        @pl.when(x % 2 != g)
        def _():
            hand_over(zz, half, p, g)

    def gather(k, carry):
        member = (m + k) % TGT_GROUP
        remote(stage.at[member], part.at[member], fin_send.at[member], fin_recv.at[member], twin).wait()
        return carry

    lax.fori_loop(1, TGT_GROUP, gather, 0)
    out = stage[m]
    for k in range(1, TGT_GROUP):
        out = out + part[(m + k) % TGT_GROUP]
    out_ref[...] = out.T[0:8, :]
    for copy in sends:
        copy.wait_send()


def shards(phase, mass, active):
    norming = 1.0 / (phase.shape[1] * lax.axis_size("row") * lax.axis_size("col"))
    vmem = pl.BlockSpec(memory_space=pltpu.VMEM)
    hbm = pl.BlockSpec(memory_space=pl.ANY)
    dma = pltpu.SemaphoreType.DMA
    sums = pl.pallas_call(
        kernel,
        out_shape=jax.ShapeDtypeStruct((8, MINE), jnp.float32),
        in_specs=[hbm, hbm, hbm],
        out_specs=vmem,
        scratch_shapes=[
            pltpu.VMEM((SRC_GROUP, 6, STARS), jnp.float32),
            pltpu.VMEM((SRC_GROUP, TILES, 128), jnp.float32),
            pltpu.VMEM((1, MINE), jnp.int32),
            pltpu.VMEM((2 * NX, 8, 128), jnp.int32),
            pltpu.VMEM((NZ, 8, 128), jnp.int32),
            pltpu.VMEM((2, 2 * NX, 2, 6, 128), jnp.float32),
            pltpu.VMEM((NZ, 2, 6, 128), jnp.float32),
            pltpu.VMEM((6, TGT_GROUP * MINE, 128), jnp.float32),
            pltpu.VMEM((2, 6, 8, 128), jnp.float32),
            pltpu.VMEM((TGT_GROUP, 8, 128), jnp.float32),
            pltpu.VMEM((TGT_GROUP, 8, 128), jnp.float32),
            dma((3,)),
            dma((15,)),
            dma((SRC_GROUP,)),
            dma((15,)),
            dma((SRC_GROUP,)),
            dma((7,)),
            dma((2 * NX,)),
            dma((7,)),
            dma((NZ,)),
            dma((7,)),
            dma((2 * NX,)),
            dma((7,)),
            dma((NZ,)),
            dma((TGT_GROUP,)),
            dma((TGT_GROUP,)),
        ],
        compiler_params=pltpu.CompilerParams(collective_id=0, has_side_effects=True),
    )(phase, mass.reshape(TILES, 128), active.reshape(1, MINE))
    return sums[0:3] * norming, sums[3:6] * norming


def solution(mesh):
    in_specs = (P(None, ("col", "row")), P(("col", "row")), P(("row", "col")))
    out_specs = (P(None, ("row", "col")), P(None, ("row", "col")))
    return jax.shard_map(shards, mesh=mesh, in_specs=in_specs, out_specs=out_specs, check_vma=False)
```

time: 69.7 us -> 63.2 us (0.907)
  the two profiles are of different devices: /device:TPU:2 before, /device:TPU:1 now
where the time goes in v3:
time: 63.2 us; the launch traced here: 62.9 us
  Pallas kernels  60.9 us (96%)
  other arithmetic  1.33 us (2%)
  between operations  0.64 us (1%)
    pallas_call x1, Pallas kernels, shards(): pl.pallas_call(kernel, out_shape=jax.ShapeDtypeStruct((8, MINE), jnp.floa...  60.9 us
    mul x1, other arithmetic, shards(): return (sums[0:3] * norming, sums[3:6] * norming)  1.33 us

profile of v3, /device:TPU:1, one launch (start us, length us, event | category | flops | bytes accessed | tf_op | source)
XLA Modules:
  0.0 62.9 jit_solution(9578708953475844597)
XLA Ops:
  0.6 60.9 %shard_map.50 = f32[8,8]{1,0:T(8,128)} custom-call(f32[6,1024]{1,0:T(8,128)} %phase_ref.1, f32[8,128]{1,0:T(8,128)} %bitcast.2, s32[1,8]{1,0:T(1,128)} %bitcast.3), custom_call_target="tpu_custom_call" | custom-call | tf_op jit(solution)/shard_map/pallas_call | solution.py:246
  61.5 1.3 %slice_multiply_fusion = (f32[3,8]{1,0:T(4,128)}, f32[3,8]{1,0:T(4,128)}) fusion(f32[8,8]{1,0:T(8,128)} %shard_map.50), kind=kLoop, calls=%fused_computation | loop fusion | flops 48 | bytes 384 | tf_op jit(solution)/shard_map/mul | solution.py:281

commit v4 on v3

--- a/solution.py
+++ b/solution.py
@@ -14,7 +14,7 @@
 STARS = 1024
 TILES = STARS // 128
 MINE = 8
-PAIRS = TGT_GROUP // 2
+BATCH = 4
 
 
 def remote(src, dst, send, recv, device):
@@ -29,33 +29,34 @@
     own_sem, src_send, src_recv, mass_send, mass_recv, ix_send, ix_recv, iz_send, iz_recv,
     px_send, px_recv, pz_send, pz_recv, fin_send, fin_recv,
 ):
+    rem, div = lax.rem, lax.div
     r, c = lax.axis_index("row"), lax.axis_index("col")
-    z_lo, b = r // 16, r % 16
-    y, core = b // 2, b % 2
-    z_hi, x = c // NX, c % NX
+    z_lo, b = div(r, 16), rem(r, 16)
+    y, core = div(b, 2), rem(b, 2)
+    z_hi, x = div(c, NX), rem(c, NX)
     z = z_hi * 2 + z_lo
     m = z_lo * 16 + c
     slot = core * NX + x
     lane = lax.broadcasted_iota(jnp.int32, (8, 128), 1)
 
     def along_y(k, dc):
-        bb = (y + k) % NY * 2 + (core + dc) % 2
+        bb = rem(y + k, NY) * 2 + (1 - core if dc else core)
         return (z_lo * 16 + bb, c), bb
 
     def along_x(k, dc):
-        xx, cc = (x + k) % NX, (core + dc) % 2
+        xx, cc = rem(x + k, NX), 1 - core if dc else core
         return (z_lo * 16 + y * 2 + cc, z_hi * NX + xx), cc * NX + xx
 
     def along_z(k):
-        zz = (z + k) % NZ
-        return (zz % 2 * 16 + b, zz // 2 * NX + x), zz
+        zz = rem(z + k, NZ)
+        return (rem(zz, 2) * 16 + b, div(zz, 2) * NX + x), zz
 
     near = [along_y(k, 0) for k in (4, 3, 5, 2, 6, 1, 7)]
     beyond = [along_y(k, 1) for k in (4, 3, 5, 2, 6, 1, 7)]
     twin, twin_block = along_y(0, 1)
     across = [along_x(k, dc) for k, dc in ((2, 1), (2, 0), (1, 1), (3, 1), (1, 0), (3, 0), (0, 1))]
     fellows = [along_z(k) for k in (4, 3, 5, 2, 6, 1, 7)]
-    partners = [d for d, _ in near + beyond + across + fellows]
+    partners = [d for d, _ in near + fellows + across]
     barrier = pltpu.get_barrier_semaphore()
     for device in partners:
         pl.semaphore_signal(barrier, inc=1, device_id=device, device_id_type=MESH)
@@ -88,8 +89,6 @@
     for n, (device, _) in enumerate(across):
         go(remote(idx_x.at[slot], idx_x.at[slot], ix_send.at[n], ix_recv.at[slot], device))
     go(remote(phase_ref, src.at[b], src_send.at[7], src_recv.at[b], twin))
-    for n, (device, _) in enumerate(near + beyond + [(twin, 0)]):
-        go(remote(mass_ref, msrc.at[b], mass_send.at[n], mass_recv.at[b], device))
 
     for device, ss in across:
         remote(idx_x.at[ss], idx_x.at[ss], ix_send.at[0], ix_recv.at[ss], device).wait_recv()
@@ -137,8 +136,11 @@
     for n in range(4):
         pick_x[n // 2, slot, n % 2] = found[n]
     for n, (device, ss) in enumerate(across):
-        cc = ss // NX
+        cc = div(ss, NX)
         go(remote(pick_x.at[cc, slot], pick_x.at[cc, slot], px_send.at[n], px_recv.at[slot], device))
+    early = len(sends)
+    for n, (device, _) in enumerate(near + beyond + [(twin, 0)]):
+        go(remote(mass_ref, msrc.at[b], mass_send.at[n], mass_recv.at[b], device))
     total = [pick_x[core, slot, q] for q in range(2)]
     for device, ss in across[::-1]:
         remote(pick_x.at[core, ss], pick_x.at[core, ss], px_send.at[0], px_recv.at[ss], device).wait_recv()
@@ -152,6 +154,8 @@
         remote(phase_ref, src.at[bb], src_send.at[0], src_recv.at[bb], twin).wait_recv()
     for device, bb in near + beyond + [(twin, twin_block)]:
         remote(mass_ref, msrc.at[bb], mass_send.at[0], mass_recv.at[bb], device).wait_recv()
+    for copy in sends[:early]:
+        copy.wait_send()
     for device, zz in fellows[::-1]:
         remote(pick_z.at[zz], pick_z.at[zz], pz_send.at[0], pz_recv.at[zz], device).wait_recv()
         for q in range(2):
@@ -161,81 +165,91 @@
         for k in range(6):
             tgt[k, q * 128:(q + 1) * 128, :] = jnp.broadcast_to(turned[:, k:k + 1], (128, 128))
 
-    def pair(i):
-        step = i // 2
-        zz = (z + 4 + (1 - 2 * (step % 2)) * ((step + 1) // 2)) % NZ
-        half = (x // 2 + 1 + i) % 2
-        return zz, half, zz % 2 * 8 + zz // 2 * 2 + half
-
-    def reduce(p):
-        for g in range(2):
-            out = jnp.zeros((8, 128), jnp.float32)
-            for n in range(6):
-                out = jnp.where(lane == n, jnp.sum(raw[g, n], axis=1, keepdims=True), out)
-            stage[p * 2 + g] = out
-
-    def hand_over(zz, half, p, g):
-        device = (zz % 2 * 16 + b, zz // 2 * NX + half * 2 + g)
-        remote(stage.at[p * 2 + g], part.at[m], fin_send.at[p * 2 + g], fin_recv.at[m], device).start()
-
-    def block(i, carry):
-        p = pair(i)[2]
-        before = pair(jnp.maximum(i - 1, 0))
-        first = pl.multiple_of(p * 16, 16)
-        here = [[tgt[k, pl.ds(first + 8 * g, 8), :] for k in range(6)] for g in range(2)]
-        reduce(before[2])
-        zero = jnp.zeros((8, 128), jnp.float32)
-        sums = [[zero] * 6, [zero] * 6]
+    def owner(i):
+        step, turn = div(i, 4), rem(i, 4)
+        zz = rem(z + 4 + (1 - 2 * rem(step, 2)) * div(step + 1, 2), NZ)
+        xx = rem(x + 2 + div(turn, 2) - rem(turn, 2) * (1 + div(turn, 2) * 2), NX)
+        return zz, xx, rem(zz, 2) * 16 + div(zz, 2) * NX + xx
+
+    def reduce(member):
+        out = jnp.zeros((8, 128), jnp.float32)
+        for n in range(6):
+            value = raw[n] if n < 3 else raw[n] - 3.0 * raw[n + 3]
+            out = jnp.where(lane == n, jnp.sum(value, axis=1, keepdims=True), out)
+        stage[member] = out
+
+    def hand_over(zz, xx, member):
+        device = (rem(zz, 2) * 16 + b, div(zz, 2) * NX + xx)
+        remote(stage.at[member], part.at[m], fin_send.at[member], fin_recv.at[m], device).start()
+
+    def sweep(member):
+        here = [tgt[k, pl.ds(pl.multiple_of(member * MINE, MINE), MINE), :] for k in range(6)]
+        sums = [jnp.zeros((8, 128), jnp.float32)] * 9
         for t in range(SRC_GROUP * TILES):
             bb, k = t // TILES, t % TILES
             star = [jnp.broadcast_to(src[bb, n:n + 1, k * 128:(k + 1) * 128], (8, 128)) for n in range(6)]
             heft = jnp.broadcast_to(msrc[bb, k:k + 1, :], (8, 128))
-            for g in range(2):
-                dx, dy, dz, du, dv, dw = (star[n] - here[g][n] for n in range(6))
-                dist_sq = (dx * dx + dy * dy + dz * dz) + SOFTENING
-                inverse = lax.rsqrt(dist_sq)
-                inverse_sq = inverse * inverse
-                weight = heft * inverse * inverse_sq
-                radial = 3.0 * (dx * du + dy * dv + dz * dw) * inverse_sq
-                s = sums[g]
-                s[0] += weight * dx
-                s[1] += weight * dy
-                s[2] += weight * dz
-                s[3] += weight * (du - radial * dx)
-                s[4] += weight * (dv - radial * dy)
-                s[5] += weight * (dw - radial * dz)
-        for g in range(2):
-            for n in range(6):
-                raw[g, n] = sums[g][n]
+            dx, dy, dz, du, dv, dw = (star[n] - here[n] for n in range(6))
+            dist_sq = (dx * dx + dy * dy + dz * dz) + SOFTENING
+            inverse = lax.rsqrt(dist_sq)
+            inverse_sq = inverse * inverse
+            weight = heft * inverse * inverse_sq
+            third = (dx * du + dy * dv + dz * dw) * inverse_sq
+            pull = (weight * dx, weight * dy, weight * dz)
+            drag = (weight * du, weight * dv, weight * dw)
+            for n in range(3):
+                sums[n] += pull[n]
+                sums[3 + n] += drag[n]
+                sums[6 + n] += third * pull[n]
+        for n in range(9):
+            raw[n] = sums[n]
+
+    def one(i, carry):
+        reduce(carry[0])
+        sweep(carry[1])
+        return carry[1], owner(i + 1)[2]
+
+    def batch(i, carry):
+        carry = lax.fori_loop(i * BATCH, i * BATCH + BATCH, one, carry)
 
         @pl.when(i > 0)
         def _():
-            for g in range(2):
-                hand_over(*before, g)
-
+            hand_over(*owner(i * BATCH - 1))
+
+        for j in range(BATCH - 1):
+            hand_over(*owner(i * BATCH + j))
         return carry
 
+    def last(i, carry):
+        before, now = carry
+        reduce(before[2])
+        hand_over(*before)
+        sweep(now[2])
+        return now, owner(i + 1)
+
     raw[...] = jnp.zeros_like(raw)
-    lax.fori_loop(0, PAIRS, block, 0)
-    zz, half, p = pair(PAIRS - 1)
-    reduce(p)
-    for g in range(2):
-        @pl.when(x % 2 != g)
-        def _():
-            hand_over(zz, half, p, g)
-
-    def gather(k, carry):
-        member = (m + k) % TGT_GROUP
-        remote(stage.at[member], part.at[member], fin_send.at[member], fin_recv.at[member], twin).wait()
+    first = owner(0)[2]
+    lax.fori_loop(0, TGT_GROUP // BATCH - 1, batch, (first, first))
+    tail = TGT_GROUP - BATCH
+    lax.fori_loop(tail, TGT_GROUP, last, (owner(tail - 1), owner(tail)))
+    reduce(m)
+
+    def sent(i, carry):
+        member = owner(i)[2]
+        remote(stage.at[member], part.at[member], fin_send.at[member], fin_recv.at[member], twin).wait_send()
         return carry
 
-    lax.fori_loop(1, TGT_GROUP, gather, 0)
-    out = stage[m]
-    for k in range(1, TGT_GROUP):
-        out = out + part[(m + k) % TGT_GROUP]
+    def arrived(i, out):
+        member = owner(i)[2]
+        remote(stage.at[member], part.at[member], fin_send.at[member], fin_recv.at[member], twin).wait_recv()
+        return out + part[member]
+
+    for copy in sends[early:]:
+        copy.wait_send()
+    lax.fori_loop(0, tail, sent, 0)
+    out = lax.fori_loop(0, TGT_GROUP - 1, arrived, stage[m])
+    lax.fori_loop(tail, TGT_GROUP - 1, sent, 0)
     out_ref[...] = out.T[0:8, :]
-    for copy in sends:
-        copy.wait_send()
 
 
 def shards(phase, mass, active):
@@ -257,7 +271,7 @@
             pltpu.VMEM((2, 2 * NX, 2, 6, 128), jnp.float32),
             pltpu.VMEM((NZ, 2, 6, 128), jnp.float32),
             pltpu.VMEM((6, TGT_GROUP * MINE, 128), jnp.float32),
-            pltpu.VMEM((2, 6, 8, 128), jnp.float32),
+            pltpu.VMEM((9, 8, 128), jnp.float32),
             pltpu.VMEM((TGT_GROUP, 8, 128), jnp.float32),
             pltpu.VMEM((TGT_GROUP, 8, 128), jnp.float32),
             dma((3,)),

time: 63.2 us -> 61.5 us (0.973)
  Pallas kernels: 60.9 us -> 59.3 us
    pallas_call x1, Pallas kernels: 60.9 us -> 59.3 us  [shards(): pl.pallas_call(kernel, out_shape=jax.ShapeDtypeStruct((8, MINE), jnp.floa...]
where the time goes in v4:
time: 61.5 us; the launch traced here: 61.3 us
  Pallas kernels  59.3 us (96%)
  other arithmetic  1.33 us (2%)
  between operations  0.64 us (1%)
    pallas_call x1, Pallas kernels, shards(): pl.pallas_call(kernel, out_shape=jax.ShapeDtypeStruct((8, MINE), jnp.floa...  59.3 us
    mul x1, other arithmetic, shards(): return (sums[0:3] * norming, sums[3:6] * norming)  1.33 us

profile of v4, /device:TPU:1, one launch (start us, length us, event | category | flops | bytes accessed | tf_op | source)
XLA Modules:
  0.0 61.3 jit_solution(13423543469576208449)
XLA Ops:
  0.6 59.3 %shard_map.50 = f32[8,8]{1,0:T(8,128)} custom-call(f32[6,1024]{1,0:T(8,128)} %phase_ref.1, f32[8,128]{1,0:T(8,128)} %bitcast.2, s32[1,8]{1,0:T(1,128)} %bitcast.3), custom_call_target="tpu_custom_call" | custom-call | tf_op jit(solution)/shard_map/pallas_call | solution.py:260
  59.9 1.3 %slice_multiply_fusion = (f32[3,8]{1,0:T(4,128)}, f32[3,8]{1,0:T(4,128)}) fusion(f32[8,8]{1,0:T(8,128)} %shard_map.50), kind=kLoop, calls=%fused_computation | loop fusion | flops 48 | bytes 384 | tf_op jit(solution)/shard_map/mul | solution.py:295

commit v5 on v4

--- a/solution.py
+++ b/solution.py
@@ -259,7 +259,7 @@
     dma = pltpu.SemaphoreType.DMA
     sums = pl.pallas_call(
         kernel,
-        out_shape=jax.ShapeDtypeStruct((8, MINE), jnp.float32),
+        out_shape=pltpu.VMEM((8, MINE), jnp.float32),
         in_specs=[hbm, hbm, hbm],
         out_specs=vmem,
         scratch_shapes=[

time: 61.5 us -> 60.1 us (0.977)
  other arithmetic: 1.33 us -> 0.59 us
    mul x1, other arithmetic: 1.33 us -> 0.59 us  [shards(): return (sums[0:3] * norming, sums[3:6] * norming)]
where the time goes in v5:
time: 60.1 us; the launch traced here: 59.9 us
  Pallas kernels  58.7 us (98%)
  between operations  0.64 us (1%)
    pallas_call x1, Pallas kernels, shards(): pl.pallas_call(kernel, out_shape=pltpu.VMEM((8, MINE), jnp.float32), in_s...  58.7 us

profile of v5, /device:TPU:1, one launch (start us, length us, event | category | flops | bytes accessed | tf_op | source)
XLA Modules:
  0.0 59.9 jit_solution(14027096132489839743)
XLA Ops:
  0.6 58.7 %shard_map.50 = f32[8,8]{1,0:T(8,128)S(1)} custom-call(f32[6,1024]{1,0:T(8,128)} %phase_ref.1, f32[8,128]{1,0:T(8,128)} %bitcast.2, s32[1,8]{1,0:T(1,128)} %bitcast.3), custom_call_target="tpu_custom_call" | custom-call | tf_op jit(solution)/shard_map/pallas_call | solution.py:260
  59.3 0.6 slice_multiply_fusion

commit v6 on v5

--- a/solution.py
+++ b/solution.py
@@ -132,7 +132,9 @@
                 found[n] = jnp.where(tile[n] == bb * TILES + k, values, found[n])
         return tuple(found)
 
-    found = lax.fori_loop(0, NY, choose, (jnp.zeros((6, 128), jnp.float32),) * 4)
+    found = (jnp.zeros((6, 128), jnp.float32),) * 4
+    for yy in range(NY):
+        found = choose(yy, found)
     for n in range(4):
         pick_x[n // 2, slot, n % 2] = found[n]
     for n, (device, ss) in enumerate(across):

time: 60.1 us -> 59.7 us (level)
  no operation moved by 1% of the time
where the time goes in v6:
time: 59.7 us; the launch traced here: 59.5 us
  Pallas kernels  58.3 us (98%)
  between operations  0.64 us (1%)
    pallas_call x1, Pallas kernels, shards(): pl.pallas_call(kernel, out_shape=pltpu.VMEM((8, MINE), jnp.float32), in_s...  58.3 us

profile of v6, /device:TPU:1, one launch (start us, length us, event | category | flops | bytes accessed | tf_op | source)
XLA Modules:
  0.0 59.5 jit_solution(9798367478600001215)
XLA Ops:
  0.6 58.3 %shard_map.50 = f32[8,8]{1,0:T(8,128)S(1)} custom-call(f32[6,1024]{1,0:T(8,128)} %phase_ref.1, f32[8,128]{1,0:T(8,128)} %bitcast.2, s32[1,8]{1,0:T(1,128)} %bitcast.3), custom_call_target="tpu_custom_call" | custom-call | tf_op jit(solution)/shard_map/pallas_call | solution.py:262
  58.9 0.6 slice_multiply_fusion
